TPU v7x, 128 devices: a whole 4x4x4 slice. The times are simulated.
128 devices in a mesh: row: 8 (over z, x_hi), col: 16 (over x_lo, y, core).
Axes of the slice: x: 4 (x_hi: 2, x_lo: 2; x = x_hi * 2 + x_lo), y: 4, z: 4, core: 2. Of those that a mesh axis runs over, the one named last changes fastest.
Arguments:
- dens_real: float32 [8192, 8192], P('row', 'col'), as said below
- dens_imag: float32 [8192, 8192], P('row', 'col'), as said below
- upper_band: float32 [8192, 384], P('row'), may hold values from -0.3 to 0.3
- pattern: int32 [64, 2], P('row'), may hold values 0 or 1
Outputs:
- new_real: float32 [8192, 8192], P('row', 'col')
- new_imag: float32 [8192, 8192], P('row', 'col')
Inputs may be any that keep to these rules, and one draw needn't show every extreme that they name: dens_real is symmetric. dens_imag is antisymmetric, with a zero diagonal.
All inputs are finite; a program needn't handle non-finite values. No bound on the sum of `pattern` on one device may be relied on, other than what follows from the above.
Results may differ from a plain program's by a relative error of at most 0.0001.
Values sent between devices are 32-bit elements; how exact they have to be, the bound alone decides.
A program may use at most 128 MiB of HBM per device.

v0:
```python
import jax
import jax.numpy as jnp
from jax import lax
from jax.experimental import pallas as pl
from jax.experimental.pallas import tpu as pltpu
from jax.sharding import PartitionSpec as P

BS = 128
KB = 2
NB = 64
STEP_TIME = 0.3
MESH = pl.DeviceIdType.MESH
F32 = jnp.float32
BF16 = jnp.bfloat16
TR = 1024
TC = 512
W = KB * BS
NG = TR // W
NJ = TC // W
ROWS = 8
COLS = 16
PIECES = [(0, BS, 2 * BS, BS), (BS, BS, BS, 2 * BS)] + [(q * BS, BS, 0, 3 * BS) for q in range(2, 6)]
LATE = (0, 1)
EARLY = (2, 3, 4, 5)


def mult(x, n=W):
    return pl.multiple_of(x, n)


def split(x):
    hi = x.astype(BF16)
    return hi, (x - hi.astype(F32)).astype(BF16)


def kernel(a_ref, b_ref, m_ref, oa_ref, ob_ref, dens, grad, xs, rowbuf, colbuf, ext, band, hrow, ncol,
           lsem, osem, rs_s, rs_r, cs_s, cs_r, ab_s, ab_r, up_s, dn_s, cr_s, bd_r):
    r, c = lax.axis_index("row"), lax.axis_index("col")
    even, core = r % 2 == 0, c % 2
    k = c // 2
    z, zk = r // 2, k // 2
    dz = (z - zk + 4) % 4
    is_src = r == k
    other = (c + 8) % 16
    crosses = r == other // 2
    fwd_up = dz < 2
    fwd_dn = dz == 0
    a_row = jnp.where(even, r + 1, r - 1)
    b_row = jnp.where(even, r - 1, r + 1)
    has_b = (b_row >= 0) & (b_row < ROWS)
    cc_col = jnp.where(core == 0, c + 1, c - 1)
    cy_col = jnp.where(core == 0, c - 1, c + 1)
    has_y = (cy_col >= 0) & (cy_col < COLS)
    z_up, z_dn = (r + 2) % ROWS, (r + 6) % ROWS
    cross_row = jnp.where(even, r + 1, r - 1)
    first = r > 0
    last = r < ROWS - 1

    row_dev = ((a_row, c), (b_row, c))
    row_src = (mult(jnp.where(even, TR - W, 0)), mult(jnp.where(even, 0, TR - W)))
    row_dst = (mult(jnp.where(even, TR + W, 0)), mult(jnp.where(even, 0, TR + W)))
    col_dev = ((r, cc_col), (r, cy_col))
    col_src = (mult(jnp.where(core == 0, TC - W, 0)), mult(jnp.where(core == 0, 0, TC - W)))
    col_dst = (mult(jnp.where(core == 0, TC + W, 0)), mult(jnp.where(core == 0, 0, TC + W)))
    g_a = jnp.where(even, NG - 1, 0)
    ext_off = mult(core * TC, BS)

    def order(t):
        return jnp.where(t < 2, t + 1, jnp.where(t == 2, g_a, NG - 1 - g_a))

    def remote(src, dst, ss, rs, dev):
        return pltpu.make_async_remote_copy(src, dst, ss, rs, device_id=dev, device_id_type=MESH)

    def row_copy(s, slot, n):
        src = (a_ref, b_ref)[n] if s == 0 else grad.at[n]
        return remote(src.at[pl.ds(row_src[slot], W), :], rowbuf.at[s, slot, n], rs_s.at[s, slot, n], rs_r.at[s, slot, n], row_dev[slot])

    def col_copy(s, slot, n, g):
        src = (a_ref, b_ref)[n] if s == 0 else grad.at[n]
        rows = pl.ds(mult(g * W), W)
        return remote(src.at[rows, pl.ds(col_src[slot], W)], colbuf.at[s, slot, n, rows, :], cs_s.at[s, slot, n, g], cs_r.at[s, slot, n, g], col_dev[slot])

    def above_copy(q):
        r0, nr, c0, nc = PIECES[q]
        return remote(m_ref.at[TR - W + r0 : TR - W + r0 + nr, c0 : c0 + nc], ext.at[r0 : r0 + nr, c0 : c0 + nc], ab_s.at[q], ab_r.at[q], (jnp.minimum(r + 1, ROWS - 1), c))

    def piece(ref, q, off=None):
        r0, nr, c0, nc = PIECES[q]
        rows = pl.ds(r0, nr) if off is None else pl.ds(mult(off + r0, BS), nr)
        return ref.at[rows, pl.ds(c0, nc)]

    def up_copy(q):
        return remote(piece(band, q), piece(band, q), up_s.at[q], bd_r.at[q], (z_up, c))

    def dn_copy(q):
        return remote(piece(band, q), piece(band, q), dn_s.at[q], bd_r.at[q], (z_dn, c))

    def cross_copy(q):
        src = piece(ext, q, ext_off) if q in LATE else piece(m_ref, q, ext_off - W)
        return remote(src, piece(band, q), cr_s.at[q], bd_r.at[q], (cross_row, other))

    def forward(q):
        @pl.when(fwd_up)
        def _():
            up_copy(q).start()

        @pl.when(fwd_dn)
        def _():
            dn_copy(q).start()

    def own_piece(q):
        src = piece(ext, q, ext_off) if q in LATE else piece(m_ref, q, ext_off - W)
        return pltpu.make_async_copy(src, piece(band, q), lsem.at[3 + q])

    barrier = pltpu.get_barrier_semaphore()

    def greet(dev):
        pl.semaphore_signal(barrier, inc=1, device_id=dev, device_id_type=MESH)

    for dev in (row_dev[0], col_dev[0], (z_up, c), (z_dn, c), (cross_row, other)):
        greet(dev)

    @pl.when(has_b)
    def _():
        greet(row_dev[1])

    @pl.when(has_y)
    def _():
        greet(col_dev[1])

    loads = [
        pltpu.make_async_copy(a_ref, dens.at[0], lsem.at[0]),
        pltpu.make_async_copy(b_ref, dens.at[1], lsem.at[1]),
        pltpu.make_async_copy(m_ref, ext.at[W:, :], lsem.at[2]),
    ]

    @pl.when(is_src)
    def _():
        for q in EARLY:
            own_piece(q).start()

    for cp in loads:
        cp.start()

    @pl.when(jnp.logical_not(first))
    def _():
        ext[0:W, :] = jnp.zeros((W, 3 * BS), F32)

    pl.semaphore_wait(barrier, 5 + has_b.astype(jnp.int32) + has_y.astype(jnp.int32))

    @pl.when(last)
    def _():
        for q in LATE:
            above_copy(q).start()

    @pl.when(crosses)
    def _():
        for q in EARLY:
            cross_copy(q).start()

    for n in range(2):
        row_copy(0, 0, n).start()

    def start_cols(s, g):
        for n in range(2):
            col_copy(s, 0, n, g).start()

        @pl.when(has_y)
        def _():
            for n in range(2):
                col_copy(s, 1, n, g).start()

    @pl.loop(0, NG)
    def _(t):
        start_cols(0, order(t))

    @pl.when(has_b)
    def _():
        for n in range(2):
            row_copy(0, 1, n).start()

    @pl.when(is_src)
    def _():
        for q in EARLY:
            own_piece(q).wait()
            forward(q)

    @pl.when(jnp.logical_not(has_b))
    def _():
        for s in range(2):
            for n in range(2):
                for p in range(2):
                    xs[s, n, p, pl.ds(row_dst[1], W), :] = jnp.zeros((W, TC + 2 * W), BF16)

    @pl.when(jnp.logical_not(has_y))
    def _():
        for s in range(2):
            for n in range(2):
                for p in range(2):
                    xs[s, n, p, :, pl.ds(col_dst[1], W)] = jnp.zeros((TR + 2 * W, W), BF16)

    loads[0].wait()
    loads[1].wait()

    @pl.loop(0, 2 * NG)
    def _(i):
        n, g = i // NG, i % NG
        hi, lo = split(dens[n, pl.ds(mult(g * W), W), :])
        xs[0, n, 0, pl.ds(mult(W + g * W), W), W : W + TC] = hi
        xs[0, n, 1, pl.ds(mult(W + g * W), W), W : W + TC] = lo

    @pl.when(jnp.logical_not(is_src))
    def _():
        for q in EARLY:
            up_copy(q).wait_recv()
            forward(q)

    loads[2].wait()

    @pl.when(first)
    def _():
        for q in LATE:
            above_copy(q).wait_recv()

    @pl.when(crosses)
    def _():
        for q in LATE:
            cross_copy(q).start()

    @pl.when(is_src)
    def _():
        for q in LATE:
            own_piece(q).start()
        for q in LATE:
            own_piece(q).wait()
            forward(q)

    @pl.loop(0, TR // BS)
    def _(i):
        g, h = i // 2, i % 2
        rows = pl.ds(mult(h * BS, BS), BS)

        def put(pos, value):
            hi, lo = split(value * STEP_TIME)
            cols = pl.ds(mult(pos * BS, BS), BS)
            hrow[0, g, rows, cols] = hi
            hrow[1, g, rows, cols] = lo

        for d in range(-KB, KB + 1):
            u = ext[pl.ds(mult((i + KB + min(d, 0)) * BS, BS), BS), abs(d) * BS : (abs(d) + 1) * BS]
            value = u if d > 0 else u.T if d < 0 else 0.5 * (u + u.T)
            put(h + d + KB, value)
        put((1 - h) * (2 * KB + 1), jnp.zeros((BS, BS), F32))

    @pl.when(jnp.logical_not(is_src))
    def _():
        for q in LATE:
            up_copy(q).wait_recv()
            forward(q)

    @pl.loop(0, TC // BS)
    def _(i):
        j, h = i // 2, i % 2
        cols = pl.ds(mult(h * BS, BS), BS)

        def put(pos, value):
            hi, lo = split(value * -STEP_TIME)
            rows = pl.ds(mult(pos * BS, BS), BS)
            ncol[0, j, rows, cols] = hi
            ncol[1, j, rows, cols] = lo

        for d in range(-KB, KB + 1):
            u = band[pl.ds(mult((i + KB + min(d, 0)) * BS, BS), BS), abs(d) * BS : (abs(d) + 1) * BS]
            value = u if d < 0 else u.T if d > 0 else 0.5 * (u + u.T)
            put(h + d + KB, value)
        put((1 - h) * (2 * KB + 1), jnp.zeros((BS, BS), F32))

    def take_cols(s, slot, g):
        rows = pl.ds(mult(g * W), W)
        for n in range(2):
            col_copy(s, slot, n, g).wait_recv()
        for n in range(2):
            hi, lo = split(colbuf[s, slot, n, rows, :])
            xs[s, n, 0, pl.ds(mult(W + g * W), W), pl.ds(col_dst[slot], W)] = hi
            xs[s, n, 1, pl.ds(mult(W + g * W), W), pl.ds(col_dst[slot], W)] = lo

    def take_rows(s, slot):
        for n in range(2):
            row_copy(s, slot, n).wait_recv()
        for n in range(2):
            hi, lo = split(rowbuf[s, slot, n])
            xs[s, n, 0, pl.ds(row_dst[slot], W), W : W + TC] = hi
            xs[s, n, 1, pl.ds(row_dst[slot], W), W : W + TC] = lo

    def product(s, n, g, j):
        r0, c0 = mult(g * W), mult(j * W)
        hi, lo = xs.at[s, 1 - n, 0], xs.at[s, 1 - n, 1]
        row_h = hi[pl.ds(r0, 3 * W), pl.ds(mult(c0 + W), W)]
        row_l = lo[pl.ds(r0, 3 * W), pl.ds(mult(c0 + W), W)]
        col_h = hi[pl.ds(mult(r0 + W), W), pl.ds(c0, 3 * W)]
        col_l = lo[pl.ds(mult(r0 + W), W), pl.ds(c0, 3 * W)]
        h_h, h_l = hrow[0, g], hrow[1, g]
        n_h, n_l = ncol[0, j], ncol[1, j]
        lhs = jnp.concatenate([h_h, h_h, h_l, col_h, col_l, col_h], axis=1)
        rhs = jnp.concatenate([row_h, row_l, row_h, n_h, n_h, n_l], axis=0)
        total = jnp.dot(lhs, rhs, preferred_element_type=F32)
        return jnp.where(n == 0, 1.0, -1.0).astype(F32) * total

    def out_copy(n, g):
        rows = pl.ds(mult(g * W), W)
        return pltpu.make_async_copy(dens.at[n, rows, :], (oa_ref, ob_ref)[n].at[rows, :], osem.at[n, g])

    for s in range(2):

        @pl.loop(0, NG)
        def _(t):
            g = order(t)
            take_cols(s, 0, g)

            @pl.when(has_y)
            def _():
                take_cols(s, 1, g)

            @pl.when(t == 2)
            def _():
                take_rows(s, 0)

            @pl.when((t == 3) & has_b)
            def _():
                take_rows(s, 1)

            @pl.loop(0, 2 * NJ)
            def _(i):
                n, j = i // NJ, i % NJ
                value = product(s, n, g, j)
                rows, cols = pl.ds(mult(g * W), W), pl.ds(mult(j * W), W)
                if s == 0:
                    grad[n, rows, cols] = value
                    hi, lo = split(value)
                    xs[1, n, 0, pl.ds(mult(W + g * W), W), pl.ds(mult(W + j * W), W)] = hi
                    xs[1, n, 1, pl.ds(mult(W + g * W), W), pl.ds(mult(W + j * W), W)] = lo
                else:
                    dens[n, rows, cols] = dens[n, rows, cols] + grad[n, rows, cols] + 0.5 * value

            if s == 0:

                @pl.when(t == 2)
                def _():
                    for n in range(2):
                        row_copy(1, 0, n).start()

                @pl.when((t == 3) & has_b)
                def _():
                    for n in range(2):
                        row_copy(1, 1, n).start()

                start_cols(1, g)
            else:
                for n in range(2):
                    out_copy(n, g).start()

    for s in range(2):
        for n in range(2):
            row_copy(s, 0, n).wait_send()

        @pl.when(has_b)
        def _():
            for n in range(2):
                row_copy(s, 1, n).wait_send()

        @pl.loop(0, NG)
        def _(g):
            for n in range(2):
                col_copy(s, 0, n, g).wait_send()

            @pl.when(has_y)
            def _():
                for n in range(2):
                    col_copy(s, 1, n, g).wait_send()

    @pl.when(last)
    def _():
        for q in LATE:
            above_copy(q).wait_send()

    @pl.when(crosses)
    def _():
        for q in range(6):
            cross_copy(q).wait_send()

    @pl.when(fwd_up)
    def _():
        for q in range(6):
            up_copy(q).wait_send()

    @pl.when(fwd_dn)
    def _():
        for q in range(6):
            dn_copy(q).wait_send()

    @pl.loop(0, NG)
    def _(g):
        for n in range(2):
            out_copy(n, g).wait()


def masked_band(upper_band, pattern, first_block):
    block_count = pattern.shape[0]
    blocks = upper_band.reshape(block_count, BS, KB + 1, BS)
    block_index = first_block + jnp.arange(block_count, dtype=jnp.int32)
    offsets = jnp.arange(1, KB + 1, dtype=jnp.int32)
    present = (pattern > 0) & (block_index[:, None] + offsets[None, :] < NB)
    present = jnp.concatenate([jnp.ones((block_count, 1), bool), present], axis=1)
    lanes = jnp.repeat(present, BS, axis=1)
    rows = jnp.repeat(lanes, BS, axis=0)
    return jnp.where(rows, upper_band, 0.0)


def shards(dens_real, dens_imag, upper_band, pattern):
    first_block = lax.axis_index("row") * (TR // BS)
    masked = masked_band(upper_band, pattern, first_block)
    dma = pltpu.SemaphoreType.DMA
    anywhere = pl.BlockSpec(memory_space=pl.ANY)
    return pl.pallas_call(
        kernel,
        out_shape=(jax.ShapeDtypeStruct((TR, TC), F32),) * 2,
        in_specs=[anywhere] * 3,
        out_specs=(anywhere,) * 2,
        scratch_shapes=[
            pltpu.VMEM((2, TR, TC), F32),
            pltpu.VMEM((2, TR, TC), F32),
            pltpu.VMEM((2, 2, 2, TR + 2 * W, TC + 2 * W), BF16),
            pltpu.VMEM((2, 2, 2, W, TC), F32),
            pltpu.VMEM((2, 2, 2, TR, W), F32),
            pltpu.VMEM((TR + W, 3 * BS), F32),
            pltpu.VMEM((TC + W, 3 * BS), F32),
            pltpu.VMEM((2, NG, W, 3 * W), BF16),
            pltpu.VMEM((2, NJ, 3 * W, W), BF16),
            dma((9,)),
            dma((2, NG)),
            dma((2, 2, 2)),
            dma((2, 2, 2)),
            dma((2, 2, 2, NG)),
            dma((2, 2, 2, NG)),
            dma((2,)),
            dma((2,)),
            dma((6,)),
            dma((6,)),
            dma((6,)),
            dma((6,)),
        ],
        compiler_params=pltpu.CompilerParams(collective_id=0, has_side_effects=True, vmem_limit_bytes=63 << 20),
        name="heun",
    )(dens_real, dens_imag, masked)


def solution(mesh):
    in_specs = (P("row", "col"), P("row", "col"), P("row", None), P("row", None))
    out_specs = (P("row", "col"), P("row", "col"))
    return jax.shard_map(shards, mesh=mesh, in_specs=in_specs, out_specs=out_specs, check_vma=False)
```

profile of v0, /device:TPU:82, one launch (start us, length us, event | category | flops | bytes accessed | tf_op | source)
XLA Modules:
  0.0 204.6 jit_solution(6167270735941363458)
XLA Ops:
  0.7 0.8 compare_and_fusion
  1.4 0.1 broadcast_bitcast_fusion
  1.5 2.7 %bitcast_select_fusion.m_ref = f32[1024,384]{1,0:T(8,128)} fusion(f32[1024,384]{1,0:T(8,128)} %param.6, pred[8,384]{1,0:T(8,128)(4,1)S(1)} %broadcast_bitcast_fusion), kind=kLoop, calls=%fused_computation | loop fusion | flops 393216 | bytes 3148800 | tf_op jit(solution)/shard_map/jit(_where)/select_n | solution.py:416
  4.2 195.9 %heun.1 = (f32[1024,512]{1,0:T(8,128)}, f32[1024,512]{1,0:T(8,128)}) custom-call(f32[1024,512]{1,0:T(8,128)} %a_ref.1, f32[1024,512]{1,0:T(8,128)} %b_ref.1, f32[1024,384]{1,0:T(8,128)} %bitcast_select_fusion.m_ref), custom_call_target="tpu_custom_call" | custom-call | tf_op jit(solution)/shard_map/heun/pallas_call | solution.py:424
  200.1 0.0 copy-start
  200.1 3.2 %copy.8 = f32[1024,512]{1,0:T(8,128)} copy(f32[1024,512]{1,0:T(8,128)} %get-tuple-element.4) | data formatting | bytes 4194304
  203.3 0.0 copy-done
  203.3 1.3 copy.9
  (3 shorter events, 0.0 us)
Async XLA Ops:
  200.1 3.2 %copy-start = (f32[1024,512]{1,0:T(8,128)S(1)}, f32[1024,512]{1,0:T(8,128)}, u32[]{:S(2)}) copy-start(f32[1024,512]{1,0:T(8,128)} %get-tuple-element.5) | copy-start | bytes 6291460
where the time goes:
time: 205 us
  Pallas kernels  196 us (96%)
  local copies, waits for them, and re-layouts  4.64 us (2%)
  other arithmetic  3.42 us (2%)
    pallas_call x1, Pallas kernels, shards(): pl.pallas_call(kernel, out_shape=(jax.ShapeDtypeStruct((TR, TC), F32),) *...  196 us
    unnamed x4, local copies, waits for them, and re-layouts  4.55 us

commit v1 on v0

--- a/solution.py
+++ b/solution.py
@@ -38,13 +38,10 @@
     r, c = lax.axis_index("row"), lax.axis_index("col")
     even, core = r % 2 == 0, c % 2
     k = c // 2
-    z, zk = r // 2, k // 2
+    z, zk, half = r // 2, k // 2, r % 2
     dz = (z - zk + 4) % 4
     is_src = r == k
-    other = (c + 8) % 16
-    crosses = r == other // 2
-    fwd_up = dz < 2
-    fwd_dn = dz == 0
+    near = half == k % 2
     a_row = jnp.where(even, r + 1, r - 1)
     b_row = jnp.where(even, r - 1, r + 1)
     has_b = (b_row >= 0) & (b_row < ROWS)
@@ -52,7 +49,6 @@
     cy_col = jnp.where(core == 0, c - 1, c + 1)
     has_y = (cy_col >= 0) & (cy_col < COLS)
     z_up, z_dn = (r + 2) % ROWS, (r + 6) % ROWS
-    cross_row = jnp.where(even, r + 1, r - 1)
     first = r > 0
     last = r < ROWS - 1
 
@@ -65,7 +61,9 @@
     g_a = jnp.where(even, NG - 1, 0)
     ext_off = mult(core * TC, BS)
 
-    def order(t):
+    def order(s, t):
+        if s == 0:
+            return jnp.where(t == 0, g_a, jnp.where(t == 3, NG - 1 - g_a, t))
         return jnp.where(t < 2, t + 1, jnp.where(t == 2, g_a, NG - 1 - g_a))
 
     def remote(src, dst, ss, rs, dev):
@@ -84,29 +82,48 @@
         r0, nr, c0, nc = PIECES[q]
         return remote(m_ref.at[TR - W + r0 : TR - W + r0 + nr, c0 : c0 + nc], ext.at[r0 : r0 + nr, c0 : c0 + nc], ab_s.at[q], ab_r.at[q], (jnp.minimum(r + 1, ROWS - 1), c))
 
-    def piece(ref, q, off=None):
-        r0, nr, c0, nc = PIECES[q]
-        rows = pl.ds(r0, nr) if off is None else pl.ds(mult(off + r0, BS), nr)
-        return ref.at[rows, pl.ds(c0, nc)]
+    def piece(ref, q, off=0):
+        if isinstance(q, int) and q in LATE:
+            r0, nr, c0, nc = PIECES[q]
+            return ref.at[pl.ds(mult(off + r0, BS), nr), c0 : c0 + nc]
+        return ref.at[pl.ds(mult(off + q * BS, BS), BS), :]
+
+    def part(q):
+        return 0 if isinstance(q, int) and q in LATE else q - 2
+
+    def hops(q):
+        return jnp.where(half == 1, dz - part(q) + 4, part(q) - dz + 4) % 4
+
+    def goes_up(q):
+        return jnp.where(near, dz < 2, (half == 1) & (hops(q) < 3))
+
+    def goes_down(q):
+        return jnp.where(near, dz == 0, (half == 0) & (hops(q) < 3))
+
+    def goes_across(q):
+        return near & (dz == part(q))
 
     def up_copy(q):
         return remote(piece(band, q), piece(band, q), up_s.at[q], bd_r.at[q], (z_up, c))
 
-    def dn_copy(q):
+    def down_copy(q):
         return remote(piece(band, q), piece(band, q), dn_s.at[q], bd_r.at[q], (z_dn, c))
 
-    def cross_copy(q):
-        src = piece(ext, q, ext_off) if q in LATE else piece(m_ref, q, ext_off - W)
-        return remote(src, piece(band, q), cr_s.at[q], bd_r.at[q], (cross_row, other))
+    def across_copy(q):
+        return remote(piece(band, q), piece(band, q), cr_s.at[q], bd_r.at[q], (a_row, c))
 
     def forward(q):
-        @pl.when(fwd_up)
+        @pl.when(goes_across(q))
+        def _():
+            across_copy(q).start()
+
+        @pl.when(goes_up(q))
         def _():
             up_copy(q).start()
 
-        @pl.when(fwd_dn)
-        def _():
-            dn_copy(q).start()
+        @pl.when(goes_down(q))
+        def _():
+            down_copy(q).start()
 
     def own_piece(q):
         src = piece(ext, q, ext_off) if q in LATE else piece(m_ref, q, ext_off - W)
@@ -117,7 +134,7 @@
     def greet(dev):
         pl.semaphore_signal(barrier, inc=1, device_id=dev, device_id_type=MESH)
 
-    for dev in (row_dev[0], col_dev[0], (z_up, c), (z_dn, c), (cross_row, other)):
+    for dev in (row_dev[0], col_dev[0], (z_up, c), (z_dn, c)):
         greet(dev)
 
     @pl.when(has_b)
@@ -146,20 +163,32 @@
     def _():
         ext[0:W, :] = jnp.zeros((W, 3 * BS), F32)
 
-    pl.semaphore_wait(barrier, 5 + has_b.astype(jnp.int32) + has_y.astype(jnp.int32))
+    pl.semaphore_wait(barrier, 4 + has_b.astype(jnp.int32) + has_y.astype(jnp.int32))
 
     @pl.when(last)
     def _():
         for q in LATE:
             above_copy(q).start()
 
-    @pl.when(crosses)
-    def _():
-        for q in EARLY:
-            cross_copy(q).start()
-
-    for n in range(2):
-        row_copy(0, 0, n).start()
+    row_copy(0, 0, 0).start()
+
+    def start_rest():
+        row_copy(0, 0, 1).start()
+
+        @pl.when(has_b)
+        def _():
+            for n in range(2):
+                row_copy(0, 1, n).start()
+
+    @pl.when(jnp.logical_not(near))
+    def _():
+        start_rest()
+
+    @pl.when(is_src)
+    def _():
+        for q in (4, 3, 5, 2):
+            own_piece(q).wait()
+            forward(q)
 
     def start_cols(s, g):
         for n in range(2):
@@ -172,18 +201,7 @@
 
     @pl.loop(0, NG)
     def _(t):
-        start_cols(0, order(t))
-
-    @pl.when(has_b)
-    def _():
-        for n in range(2):
-            row_copy(0, 1, n).start()
-
-    @pl.when(is_src)
-    def _():
-        for q in EARLY:
-            own_piece(q).wait()
-            forward(q)
+        start_cols(0, order(0, t))
 
     @pl.when(jnp.logical_not(has_b))
     def _():
@@ -209,31 +227,37 @@
         xs[0, n, 0, pl.ds(mult(W + g * W), W), W : W + TC] = hi
         xs[0, n, 1, pl.ds(mult(W + g * W), W), W : W + TC] = lo
 
-    @pl.when(jnp.logical_not(is_src))
-    def _():
-        for q in EARLY:
-            up_copy(q).wait_recv()
-            forward(q)
-
     loads[2].wait()
 
-    @pl.when(first)
-    def _():
-        for q in LATE:
-            above_copy(q).wait_recv()
-
-    @pl.when(crosses)
-    def _():
-        for q in LATE:
-            cross_copy(q).start()
-
     @pl.when(is_src)
     def _():
+        @pl.when(first)
+        def _():
+            for q in LATE:
+                above_copy(q).wait_recv()
+
         for q in LATE:
             own_piece(q).start()
         for q in LATE:
             own_piece(q).wait()
             forward(q)
+        start_rest()
+
+    @pl.when(jnp.logical_not(is_src))
+    def _():
+        for e in range(4):
+            q = 2 + jnp.where(near, (2, 1, 3, 0)[e], jnp.where(half == 1, dz - e + 4, dz + e) % 4)
+            up_copy(q).wait_recv()
+            forward(q)
+
+            @pl.when(goes_across(q))
+            def _():
+                start_rest()
+
+        @pl.when(first)
+        def _():
+            for q in LATE:
+                above_copy(q).wait_recv()
 
     @pl.loop(0, TR // BS)
     def _(i):
@@ -314,14 +338,14 @@
 
         @pl.loop(0, NG)
         def _(t):
-            g = order(t)
+            g = order(s, t)
             take_cols(s, 0, g)
 
             @pl.when(has_y)
             def _():
                 take_cols(s, 1, g)
 
-            @pl.when(t == 2)
+            @pl.when(t == 2 * s)
             def _():
                 take_rows(s, 0)
 
@@ -344,7 +368,7 @@
 
             if s == 0:
 
-                @pl.when(t == 2)
+                @pl.when(t == 0)
                 def _():
                     for n in range(2):
                         row_copy(1, 0, n).start()
@@ -383,20 +407,19 @@
         for q in LATE:
             above_copy(q).wait_send()
 
-    @pl.when(crosses)
-    def _():
-        for q in range(6):
-            cross_copy(q).wait_send()
-
-    @pl.when(fwd_up)
-    def _():
-        for q in range(6):
+    for q in range(6):
+
+        @pl.when(goes_across(q))
+        def _():
+            across_copy(q).wait_send()
+
+        @pl.when(goes_up(q))
+        def _():
             up_copy(q).wait_send()
 
-    @pl.when(fwd_dn)
-    def _():
-        for q in range(6):
-            dn_copy(q).wait_send()
+        @pl.when(goes_down(q))
+        def _():
+            down_copy(q).wait_send()
 
     @pl.loop(0, NG)
     def _(g):

time: 205 us -> 168 us (0.82)
  the two profiles are of different devices: /device:TPU:82 before, /device:TPU:6 now
where the time goes in v1:
time: 168 us; the launch traced here: 166 us
  Pallas kernels  157 us (93%)
  local copies, waits for them, and re-layouts  4.64 us (3%)
  other arithmetic  3.42 us (2%)
    pallas_call x1, Pallas kernels, shards(): pl.pallas_call(kernel, out_shape=(jax.ShapeDtypeStruct((TR, TC), F32),) *...  157 us
    unnamed x4, local copies, waits for them, and re-layouts  4.55 us

profile of v1, /device:TPU:6, one launch (start us, length us, event | category | flops | bytes accessed | tf_op | source)
XLA Modules:
  0.0 165.6 jit_solution(12154156104140273904)
XLA Ops:
  0.7 0.8 compare_and_fusion
  1.4 0.1 broadcast_bitcast_fusion
  1.5 2.7 %bitcast_select_fusion.m_ref = f32[1024,384]{1,0:T(8,128)} fusion(f32[1024,384]{1,0:T(8,128)} %param.6, pred[8,384]{1,0:T(8,128)(4,1)S(1)} %broadcast_bitcast_fusion), kind=kLoop, calls=%fused_computation | loop fusion | flops 393216 | bytes 3148800 | tf_op jit(solution)/shard_map/jit(_where)/select_n | solution.py:439
  4.2 156.8 %heun.1 = (f32[1024,512]{1,0:T(8,128)}, f32[1024,512]{1,0:T(8,128)}) custom-call(f32[1024,512]{1,0:T(8,128)} %a_ref.1, f32[1024,512]{1,0:T(8,128)} %b_ref.1, f32[1024,384]{1,0:T(8,128)} %bitcast_select_fusion.m_ref), custom_call_target="tpu_custom_call" | custom-call | tf_op jit(solution)/shard_map/heun/pallas_call | solution.py:447
  161.0 0.0 copy-start
  161.0 3.2 %copy.8 = f32[1024,512]{1,0:T(8,128)} copy(f32[1024,512]{1,0:T(8,128)} %get-tuple-element.4) | data formatting | bytes 4194304
  164.2 0.0 copy-done
  164.2 1.3 copy.9
  (3 shorter events, 0.0 us)
Async XLA Ops:
  161.0 3.2 %copy-start = (f32[1024,512]{1,0:T(8,128)S(1)}, f32[1024,512]{1,0:T(8,128)}, u32[]{:S(2)}) copy-start(f32[1024,512]{1,0:T(8,128)} %get-tuple-element.5) | copy-start | bytes 6291460

commit v2 on v1

--- a/solution.py
+++ b/solution.py
@@ -33,8 +33,8 @@
     return hi, (x - hi.astype(F32)).astype(BF16)
 
 
-def kernel(a_ref, b_ref, m_ref, oa_ref, ob_ref, dens, grad, xs, rowbuf, colbuf, ext, band, hrow, ncol,
-           lsem, osem, rs_s, rs_r, cs_s, cs_r, ab_s, ab_r, up_s, dn_s, cr_s, bd_r):
+def kernel(a_ref, b_ref, u_ref, pat_ref, dens, grad, xs, rowbuf, colbuf, ext, band, hrow, ncol, relay,
+           lsem, rs_s, rs_r, cs_s, cs_r, ab_s, ab_r, up_s, dn_s, cr_s, bd_r, rl_s, rl_r):
     r, c = lax.axis_index("row"), lax.axis_index("col")
     even, core = r % 2 == 0, c % 2
     k = c // 2
@@ -48,6 +48,11 @@
     cc_col = jnp.where(core == 0, c + 1, c - 1)
     cy_col = jnp.where(core == 0, c - 1, c + 1)
     has_y = (cy_col >= 0) & (cy_col < COLS)
+    hub = (c == 7) | (c == 8)
+    mine = jnp.minimum(c, COLS - 1 - c)
+    is_relay = (mine % 2 == 0) & (mine < 6)
+    relay_turn = jnp.where(mine == 0, 1, jnp.where(mine == 4, 2, 3))
+    relay_to = jnp.where(c < 8, 8, 7)
     z_up, z_dn = (r + 2) % ROWS, (r + 6) % ROWS
     first = r > 0
     last = r < ROWS - 1
@@ -78,9 +83,28 @@
         rows = pl.ds(mult(g * W), W)
         return remote(src.at[rows, pl.ds(col_src[slot], W)], colbuf.at[s, slot, n, rows, :], cs_s.at[s, slot, n, g], cs_r.at[s, slot, n, g], col_dev[slot])
 
+    def hub_copy(s, n, t):
+        g = order(0, t)
+        src = (a_ref, b_ref)[n] if s == 0 else grad.at[n]
+        near_col = jnp.where(t == 1, 0, jnp.where(t == 2, 4, 2))
+        to = jnp.where(c < 8, near_col, COLS - 1 - near_col)
+        return remote(src.at[pl.ds(mult(g * W), W), pl.ds(col_src[1], W)], relay.at[s, n], cs_s.at[s, 1, n, g], rl_r.at[s, n], (r, to))
+
+    def relay_copy(s, n):
+        g = order(0, relay_turn)
+        return remote(relay.at[s, n], colbuf.at[s, 1, n, pl.ds(mult(g * W), W), :], rl_s.at[s, n], cs_r.at[s, 1, n, g], (r, relay_to))
+
+    def pass_on(s):
+        @pl.when(is_relay)
+        def _():
+            for n in range(2):
+                hub_copy(s, n, 1).wait_recv()
+            for n in range(2):
+                relay_copy(s, n).start()
+
     def above_copy(q):
         r0, nr, c0, nc = PIECES[q]
-        return remote(m_ref.at[TR - W + r0 : TR - W + r0 + nr, c0 : c0 + nc], ext.at[r0 : r0 + nr, c0 : c0 + nc], ab_s.at[q], ab_r.at[q], (jnp.minimum(r + 1, ROWS - 1), c))
+        return remote(ext.at[TR + r0 : TR + r0 + nr, c0 : c0 + nc], ext.at[r0 : r0 + nr, c0 : c0 + nc], ab_s.at[q], ab_r.at[q], (jnp.minimum(r + 1, ROWS - 1), c))
 
     def piece(ref, q, off=0):
         if isinstance(q, int) and q in LATE:
@@ -126,8 +150,7 @@
             down_copy(q).start()
 
     def own_piece(q):
-        src = piece(ext, q, ext_off) if q in LATE else piece(m_ref, q, ext_off - W)
-        return pltpu.make_async_copy(src, piece(band, q), lsem.at[3 + q])
+        return pltpu.make_async_copy(piece(ext, q, ext_off), piece(band, q), lsem.at[3 + q])
 
     barrier = pltpu.get_barrier_semaphore()
 
@@ -148,22 +171,42 @@
     loads = [
         pltpu.make_async_copy(a_ref, dens.at[0], lsem.at[0]),
         pltpu.make_async_copy(b_ref, dens.at[1], lsem.at[1]),
-        pltpu.make_async_copy(m_ref, ext.at[W:, :], lsem.at[2]),
+        pltpu.make_async_copy(u_ref, ext.at[W:, :], lsem.at[2]),
     ]
+
+    for cp in loads[::-1]:
+        cp.start()
+
+    @pl.when(jnp.logical_not(first))
+    def _():
+        ext[0:W, :] = jnp.zeros((W, 3 * BS), F32)
+
+    loads[2].wait()
+
+    @pl.loop(0, TR // BS)
+    def _(i):
+        rows = pl.ds(mult(W + i * BS, BS), BS)
+        for d in range(1, KB + 1):
+            present = (pat_ref[i, d - 1] > 0) & (r * (TR // BS) + i + d < NB)
+            cols = slice(d * BS, (d + 1) * BS)
+            ext[rows, cols] = ext[rows, cols] * jnp.where(present, 1.0, 0.0).astype(F32)
 
     @pl.when(is_src)
     def _():
         for q in EARLY:
             own_piece(q).start()
 
-    for cp in loads:
-        cp.start()
-
-    @pl.when(jnp.logical_not(first))
-    def _():
-        ext[0:W, :] = jnp.zeros((W, 3 * BS), F32)
-
-    pl.semaphore_wait(barrier, 4 + has_b.astype(jnp.int32) + has_y.astype(jnp.int32))
+    @pl.when(hub)
+    def _():
+        for col in (0, 2, 4, 11, 13, 15):
+            greet((r, col))
+
+    @pl.when(is_relay)
+    def _():
+        for col in (7, 8):
+            greet((r, col))
+
+    pl.semaphore_wait(barrier, 4 + has_b.astype(jnp.int32) + has_y.astype(jnp.int32) + jnp.where(hub, 6, 0) + jnp.where(is_relay, 2, 0))
 
     @pl.when(last)
     def _():
@@ -172,17 +215,17 @@
 
     row_copy(0, 0, 0).start()
 
-    def start_rest():
+    def start_b():
+        pass_on(0)
+
+        @pl.when(has_b)
+        def _():
+            for n in range(2):
+                row_copy(0, 1, n).start()
+
+    @pl.when(jnp.logical_not(near))
+    def _():
         row_copy(0, 0, 1).start()
-
-        @pl.when(has_b)
-        def _():
-            for n in range(2):
-                row_copy(0, 1, n).start()
-
-    @pl.when(jnp.logical_not(near))
-    def _():
-        start_rest()
 
     @pl.when(is_src)
     def _():
@@ -190,25 +233,35 @@
             own_piece(q).wait()
             forward(q)
 
-    def start_cols(s, g):
+    def start_cols(s, t):
+        g = order(0, t)
         for n in range(2):
             col_copy(s, 0, n, g).start()
 
-        @pl.when(has_y)
+        @pl.when(has_y & (jnp.logical_not(hub) | (t == 0)))
         def _():
             for n in range(2):
                 col_copy(s, 1, n, g).start()
+
+        @pl.when(hub & (t > 0))
+        def _():
+            for n in range(2):
+                hub_copy(s, n, t).start()
 
     @pl.loop(0, NG)
     def _(t):
-        start_cols(0, order(0, t))
+        start_cols(0, t)
+
+    def clear_rows(s):
+        for n in range(2):
+            for p in range(2):
+                xs[s, n, p, pl.ds(row_dst[1], W), W : W + TC] = jnp.zeros((W, TC), BF16)
 
     @pl.when(jnp.logical_not(has_b))
     def _():
-        for s in range(2):
-            for n in range(2):
-                for p in range(2):
-                    xs[s, n, p, pl.ds(row_dst[1], W), :] = jnp.zeros((W, TC + 2 * W), BF16)
+        clear_rows(0)
+
+    clear_rows(1)
 
     @pl.when(jnp.logical_not(has_y))
     def _():
@@ -227,8 +280,6 @@
         xs[0, n, 0, pl.ds(mult(W + g * W), W), W : W + TC] = hi
         xs[0, n, 1, pl.ds(mult(W + g * W), W), W : W + TC] = lo
 
-    loads[2].wait()
-
     @pl.when(is_src)
     def _():
         @pl.when(first)
@@ -241,7 +292,12 @@
         for q in LATE:
             own_piece(q).wait()
             forward(q)
-        start_rest()
+        row_copy(0, 0, 1).start()
+        start_b()
+
+    @pl.when(jnp.logical_not(near))
+    def _():
+        start_b()
 
     @pl.when(jnp.logical_not(is_src))
     def _():
@@ -252,7 +308,13 @@
 
             @pl.when(goes_across(q))
             def _():
-                start_rest()
+                row_copy(0, 0, 1).start()
+
+            if e == 2:
+
+                @pl.when(near)
+                def _():
+                    start_b()
 
         @pl.when(first)
         def _():
@@ -330,9 +392,16 @@
         total = jnp.dot(lhs, rhs, preferred_element_type=F32)
         return jnp.where(n == 0, 1.0, -1.0).astype(F32) * total
 
-    def out_copy(n, g):
+    def last_part(n):
+        g = NG - 1 - g_a
+        row_copy(1, 1, n).wait_recv()
+        hi, lo = split(rowbuf[1, 1, n])
+        cols = pl.ds(mult(jnp.where(even, 0, 2 * W)), W)
+        h_h, h_l = hrow[0, g, :, cols], hrow[1, g, :, cols]
+        lhs = jnp.concatenate([h_h, h_h, h_l], axis=1)
+        rhs = jnp.concatenate([hi, lo, hi], axis=0)
         rows = pl.ds(mult(g * W), W)
-        return pltpu.make_async_copy(dens.at[n, rows, :], (oa_ref, ob_ref)[n].at[rows, :], osem.at[n, g])
+        dens[1 - n, rows, :] += (-0.5 if n == 0 else 0.5) * jnp.dot(lhs, rhs, preferred_element_type=F32)
 
     for s in range(2):
 
@@ -349,9 +418,11 @@
             def _():
                 take_rows(s, 0)
 
-            @pl.when((t == 3) & has_b)
-            def _():
-                take_rows(s, 1)
+            if s == 0:
+
+                @pl.when((t == 3) & has_b)
+                def _():
+                    take_rows(s, 1)
 
             @pl.loop(0, 2 * NJ)
             def _(i):
@@ -373,15 +444,21 @@
                     for n in range(2):
                         row_copy(1, 0, n).start()
 
+                start_cols(1, t)
+
+                @pl.when(t == 3)
+                def _():
+                    pass_on(1)
+
                 @pl.when((t == 3) & has_b)
                 def _():
                     for n in range(2):
                         row_copy(1, 1, n).start()
 
-                start_cols(1, g)
-            else:
-                for n in range(2):
-                    out_copy(n, g).start()
+    @pl.when(has_b)
+    def _():
+        for n in range(2):
+            last_part(n)
 
     for s in range(2):
         for n in range(2):
@@ -402,6 +479,12 @@
                 for n in range(2):
                     col_copy(s, 1, n, g).wait_send()
 
+    @pl.when(is_relay)
+    def _():
+        for s in range(2):
+            for n in range(2):
+                relay_copy(s, n).wait_send()
+
     @pl.when(last)
     def _():
         for q in LATE:
@@ -421,36 +504,16 @@
         def _():
             down_copy(q).wait_send()
 
-    @pl.loop(0, NG)
-    def _(g):
-        for n in range(2):
-            out_copy(n, g).wait()
-
-
-def masked_band(upper_band, pattern, first_block):
-    block_count = pattern.shape[0]
-    blocks = upper_band.reshape(block_count, BS, KB + 1, BS)
-    block_index = first_block + jnp.arange(block_count, dtype=jnp.int32)
-    offsets = jnp.arange(1, KB + 1, dtype=jnp.int32)
-    present = (pattern > 0) & (block_index[:, None] + offsets[None, :] < NB)
-    present = jnp.concatenate([jnp.ones((block_count, 1), bool), present], axis=1)
-    lanes = jnp.repeat(present, BS, axis=1)
-    rows = jnp.repeat(lanes, BS, axis=0)
-    return jnp.where(rows, upper_band, 0.0)
-
 
 def shards(dens_real, dens_imag, upper_band, pattern):
-    first_block = lax.axis_index("row") * (TR // BS)
-    masked = masked_band(upper_band, pattern, first_block)
     dma = pltpu.SemaphoreType.DMA
     anywhere = pl.BlockSpec(memory_space=pl.ANY)
-    return pl.pallas_call(
+    out = pl.pallas_call(
         kernel,
-        out_shape=(jax.ShapeDtypeStruct((TR, TC), F32),) * 2,
-        in_specs=[anywhere] * 3,
-        out_specs=(anywhere,) * 2,
+        out_shape=pltpu.VMEM((2, TR, TC), F32),
+        in_specs=[anywhere] * 3 + [pl.BlockSpec(memory_space=pltpu.SMEM)],
+        out_specs=pl.BlockSpec(memory_space=pltpu.VMEM),
         scratch_shapes=[
-            pltpu.VMEM((2, TR, TC), F32),
             pltpu.VMEM((2, TR, TC), F32),
             pltpu.VMEM((2, 2, 2, TR + 2 * W, TC + 2 * W), BF16),
             pltpu.VMEM((2, 2, 2, W, TC), F32),
@@ -459,8 +522,8 @@
             pltpu.VMEM((TC + W, 3 * BS), F32),
             pltpu.VMEM((2, NG, W, 3 * W), BF16),
             pltpu.VMEM((2, NJ, 3 * W, W), BF16),
+            pltpu.VMEM((2, 2, W, W), F32),
             dma((9,)),
-            dma((2, NG)),
             dma((2, 2, 2)),
             dma((2, 2, 2)),
             dma((2, 2, 2, NG)),
@@ -471,10 +534,13 @@
             dma((6,)),
             dma((6,)),
             dma((6,)),
+            dma((2, 2)),
+            dma((2, 2)),
         ],
-        compiler_params=pltpu.CompilerParams(collective_id=0, has_side_effects=True, vmem_limit_bytes=63 << 20),
+        compiler_params=pltpu.CompilerParams(collective_id=0, has_side_effects=True, vmem_limit_bytes=55 << 20),
         name="heun",
-    )(dens_real, dens_imag, masked)
+    )(dens_real, dens_imag, upper_band, pattern)
+    return out[0], out[1]
 
 
 def solution(mesh):

time: 168 us -> 128 us (0.76)
  the two profiles are of different devices: /device:TPU:6 before, /device:TPU:40 now
where the time goes in v2:
time: 128 us
  Pallas kernels  123 us (96%)
  local copies, waits for them, and re-layouts  3.79 us (3%)
    pallas_call x1, Pallas kernels, shards(): pl.pallas_call(kernel, out_shape=pltpu.VMEM((2, TR, TC), F32), in_specs=[...  123 us

profile of v2, /device:TPU:40, one launch (start us, length us, event | category | flops | bytes accessed | tf_op | source)
XLA Modules:
  0.0 127.7 jit_solution(10499375722856738349)
XLA Ops:
  0.6 1.3 %copy.6.pat_ref = s32[8,2]{1,0:T(8,128)} copy(s32[8,2]{0,1:T(2,128)} %param.7) | data formatting | bytes 128 | tf_op args[3]
  2.0 123.2 %heun.1 = f32[2,1024,512]{2,1,0:T(8,128)S(1)} custom-call(f32[1024,512]{1,0:T(8,128)} %a_ref.1, f32[1024,512]{1,0:T(8,128)} %b_ref.1, f32[1024,384]{1,0:T(8,128)} %u_ref.1, s32[8,2]{1,0:T(8,128)} %copy.6.pat_ref), custom_call_target="tpu_custom_call" | custom-call | tf_op jit(solution)/shard_map/heun/pallas_call | solution.py:511
  125.2 2.4 %slice_bitcast_fusion = (f32[1024,512]{1,0:T(8,128)}, f32[1024,512]{1,0:T(8,128)}) fusion(f32[2,1024,512]{2,1,0:T(8,128)S(1)} %heun.1), kind=kLoop, calls=%fused_computation | loop fusion | bytes 8388608 | tf_op jit(solution)/shard_map/squeeze | solution.py:543

commit v3 on v2

--- a/solution.py
+++ b/solution.py
@@ -33,13 +33,15 @@
     return hi, (x - hi.astype(F32)).astype(BF16)
 
 
-def kernel(a_ref, b_ref, u_ref, pat_ref, dens, grad, xs, rowbuf, colbuf, ext, band, hrow, ncol, relay,
-           lsem, rs_s, rs_r, cs_s, cs_r, ab_s, ab_r, up_s, dn_s, cr_s, bd_r, rl_s, rl_r):
+def kernel(a_ref, b_ref, u_ref, pat_ref, dens, grad, xs, rowbuf, colbuf, ext, band, hrow, ncol, relay, zrelay,
+           lsem, rs_s, rs_r, bs_s, bs_r, bz_s, bz_r, cs_s, cs_r, ab_s, ab_r, al_s, cr_s, bd_r, rl_s, rl_r):
     r, c = lax.axis_index("row"), lax.axis_index("col")
     even, core = r % 2 == 0, c % 2
     k = c // 2
     z, zk, half = r // 2, k // 2, r % 2
-    dz = (z - zk + 4) % 4
+    step_up = k % 2 == 0
+    dist = jnp.where(step_up, z - zk, zk - z)
+    dist = (dist + 4) % 4
     is_src = r == k
     near = half == k % 2
     a_row = jnp.where(even, r + 1, r - 1)
@@ -54,6 +56,10 @@
     relay_turn = jnp.where(mine == 0, 1, jnp.where(mine == 4, 2, 3))
     relay_to = jnp.where(c < 8, 8, 7)
     z_up, z_dn = (r + 2) % ROWS, (r + 6) % ROWS
+    z_next = jnp.where(step_up, z_up, z_dn)
+    depth = jnp.where(even, z, 3 - z)
+    first_far = depth
+    z_relay = jnp.where(even, z_dn, z_up)
     first = r > 0
     last = r < ROWS - 1
 
@@ -74,9 +80,47 @@
     def remote(src, dst, ss, rs, dev):
         return pltpu.make_async_remote_copy(src, dst, ss, rs, device_id=dev, device_id_type=MESH)
 
-    def row_copy(s, slot, n):
+    def row_copy(s, n):
         src = (a_ref, b_ref)[n] if s == 0 else grad.at[n]
-        return remote(src.at[pl.ds(row_src[slot], W), :], rowbuf.at[s, slot, n], rs_s.at[s, slot, n], rs_r.at[s, slot, n], row_dev[slot])
+        return remote(src.at[pl.ds(row_src[0], W), :], rowbuf.at[s, 0, n], rs_s.at[s, n], rs_r.at[s, n], row_dev[0])
+
+    def b_src(s, i):
+        src = (a_ref, b_ref)[i // 2] if s == 0 else grad.at[i // 2]
+        return src.at[pl.ds(mult(row_src[1] + i % 2 * BS, BS), BS), :]
+
+    def b_dst(s, i):
+        return rowbuf.at[s, 1, i // 2, i % 2 * BS : (i % 2 + 1) * BS, :]
+
+    def b_direct(s, i):
+        return remote(b_src(s, i), b_dst(s, i), bs_s.at[s, i], bs_r.at[s, i], row_dev[1])
+
+    def b_first(s, i):
+        return remote(b_src(s, i), zrelay.at[s, i], bs_s.at[s, i], bz_r.at[s, i], (z_relay, c))
+
+    def b_second(s, i):
+        return remote(zrelay.at[s, i], b_dst(s, i), bz_s.at[s, i], bs_r.at[s, i], (a_row, c))
+
+    def b_far(s):
+        for i in range(4):
+
+            @pl.when(has_b & (i >= first_far))
+            def _():
+                b_first(s, i).start()
+
+    def b_near(s):
+        for i in range(3):
+
+            @pl.when(has_b & (i < first_far))
+            def _():
+                b_direct(s, i).start()
+
+    def b_pass(s):
+        for i in range(1, 4):
+
+            @pl.when(i > depth)
+            def _():
+                b_first(s, i).wait_recv()
+                b_second(s, i).start()
 
     def col_copy(s, slot, n, g):
         src = (a_ref, b_ref)[n] if s == 0 else grad.at[n]
@@ -94,8 +138,8 @@
         g = order(0, relay_turn)
         return remote(relay.at[s, n], colbuf.at[s, 1, n, pl.ds(mult(g * W), W), :], rl_s.at[s, n], cs_r.at[s, 1, n, g], (r, relay_to))
 
-    def pass_on(s):
-        @pl.when(is_relay)
+    def pass_on(s, turns):
+        @pl.when(is_relay & ((relay_turn == 3) == (turns == 3)))
         def _():
             for n in range(2):
                 hub_copy(s, n, 1).wait_recv()
@@ -116,38 +160,31 @@
         return 0 if isinstance(q, int) and q in LATE else q - 2
 
     def hops(q):
-        return jnp.where(half == 1, dz - part(q) + 4, part(q) - dz + 4) % 4
-
-    def goes_up(q):
-        return jnp.where(near, dz < 2, (half == 1) & (hops(q) < 3))
-
-    def goes_down(q):
-        return jnp.where(near, dz == 0, (half == 0) & (hops(q) < 3))
+        return (dist - part(q) + 4) % 4
+
+    def goes_along(q):
+        return jnp.where(near, dist, hops(q)) < 3
 
     def goes_across(q):
-        return near & (dz == part(q))
-
-    def up_copy(q):
-        return remote(piece(band, q), piece(band, q), up_s.at[q], bd_r.at[q], (z_up, c))
-
-    def down_copy(q):
-        return remote(piece(band, q), piece(band, q), dn_s.at[q], bd_r.at[q], (z_dn, c))
+        return near & (dist == part(q))
+
+    def along_copy(q):
+        return remote(piece(band, q), piece(band, q), al_s.at[q], bd_r.at[q], (z_next, c))
 
     def across_copy(q):
         return remote(piece(band, q), piece(band, q), cr_s.at[q], bd_r.at[q], (a_row, c))
 
+    def along(q):
+        @pl.when(goes_along(q))
+        def _():
+            along_copy(q).start()
+
     def forward(q):
         @pl.when(goes_across(q))
         def _():
             across_copy(q).start()
 
-        @pl.when(goes_up(q))
-        def _():
-            up_copy(q).start()
-
-        @pl.when(goes_down(q))
-        def _():
-            down_copy(q).start()
+        along(q)
 
     def own_piece(q):
         return pltpu.make_async_copy(piece(ext, q, ext_off), piece(band, q), lsem.at[3 + q])
@@ -213,25 +250,30 @@
         for q in LATE:
             above_copy(q).start()
 
-    row_copy(0, 0, 0).start()
-
     def start_b():
-        pass_on(0)
-
-        @pl.when(has_b)
-        def _():
-            for n in range(2):
-                row_copy(0, 1, n).start()
+        pass_on(0, 1)
+        b_near(0)
+        b_pass(0)
+
+    @pl.when(is_src)
+    def _():
+        own_piece(2).wait()
+        across_copy(2).start()
+
+    row_copy(0, 0).start()
 
     @pl.when(jnp.logical_not(near))
     def _():
-        row_copy(0, 0, 1).start()
+        row_copy(0, 1).start()
+
+    b_far(0)
 
     @pl.when(is_src)
     def _():
-        for q in (4, 3, 5, 2):
+        for q in (5, 4, 3):
             own_piece(q).wait()
-            forward(q)
+            along(q)
+        along(2)
 
     def start_cols(s, t):
         g = order(0, t)
@@ -292,34 +334,36 @@
         for q in LATE:
             own_piece(q).wait()
             forward(q)
-        row_copy(0, 0, 1).start()
+        row_copy(0, 1).start()
         start_b()
 
-    @pl.when(jnp.logical_not(near))
-    def _():
-        start_b()
-
     @pl.when(jnp.logical_not(is_src))
     def _():
         for e in range(4):
-            q = 2 + jnp.where(near, (2, 1, 3, 0)[e], jnp.where(half == 1, dz - e + 4, dz + e) % 4)
-            up_copy(q).wait_recv()
+            q = 2 + jnp.where(near, 3 - e, (dist - e + 4) % 4)
+            along_copy(q).wait_recv()
             forward(q)
 
             @pl.when(goes_across(q))
             def _():
-                row_copy(0, 0, 1).start()
-
-            if e == 2:
-
-                @pl.when(near)
-                def _():
-                    start_b()
+                row_copy(0, 1).start()
+
+            @pl.when(e == jnp.where(near, 2, 0))
+            def _():
+                start_b()
+
+            @pl.when(e == jnp.where(near, 3, dist))
+            def _():
+                for p in LATE:
+                    along_copy(p).wait_recv()
+                    forward(p)
 
         @pl.when(first)
         def _():
             for q in LATE:
                 above_copy(q).wait_recv()
+
+    pass_on(0, 3)
 
     @pl.loop(0, TR // BS)
     def _(i):
@@ -338,12 +382,6 @@
             put(h + d + KB, value)
         put((1 - h) * (2 * KB + 1), jnp.zeros((BS, BS), F32))
 
-    @pl.when(jnp.logical_not(is_src))
-    def _():
-        for q in LATE:
-            up_copy(q).wait_recv()
-            forward(q)
-
     @pl.loop(0, TC // BS)
     def _(i):
         j, h = i // 2, i % 2
@@ -371,8 +409,12 @@
             xs[s, n, 1, pl.ds(mult(W + g * W), W), pl.ds(col_dst[slot], W)] = lo
 
     def take_rows(s, slot):
-        for n in range(2):
-            row_copy(s, slot, n).wait_recv()
+        if slot == 0:
+            for n in range(2):
+                row_copy(s, n).wait_recv()
+        else:
+            for i in range(4):
+                b_direct(s, i).wait_recv()
         for n in range(2):
             hi, lo = split(rowbuf[s, slot, n])
             xs[s, n, 0, pl.ds(row_dst[slot], W), W : W + TC] = hi
@@ -394,7 +436,8 @@
 
     def last_part(n):
         g = NG - 1 - g_a
-        row_copy(1, 1, n).wait_recv()
+        for i in (2 * n, 2 * n + 1):
+            b_direct(1, i).wait_recv()
         hi, lo = split(rowbuf[1, 1, n])
         cols = pl.ds(mult(jnp.where(even, 0, 2 * W)), W)
         h_h, h_l = hrow[0, g, :, cols], hrow[1, g, :, cols]
@@ -442,18 +485,17 @@
                 @pl.when(t == 0)
                 def _():
                     for n in range(2):
-                        row_copy(1, 0, n).start()
+                        row_copy(1, n).start()
 
                 start_cols(1, t)
 
                 @pl.when(t == 3)
                 def _():
-                    pass_on(1)
-
-                @pl.when((t == 3) & has_b)
-                def _():
-                    for n in range(2):
-                        row_copy(1, 1, n).start()
+                    b_far(1)
+                    pass_on(1, 1)
+                    b_near(1)
+                    b_pass(1)
+                    pass_on(1, 3)
 
     @pl.when(has_b)
     def _():
@@ -462,12 +504,18 @@
 
     for s in range(2):
         for n in range(2):
-            row_copy(s, 0, n).wait_send()
+            row_copy(s, n).wait_send()
 
         @pl.when(has_b)
         def _():
-            for n in range(2):
-                row_copy(s, 1, n).wait_send()
+            for i in range(4):
+                b_direct(s, i).wait_send()
+
+        for i in range(1, 4):
+
+            @pl.when(i > depth)
+            def _():
+                b_second(s, i).wait_send()
 
         @pl.loop(0, NG)
         def _(g):
@@ -496,13 +544,9 @@
         def _():
             across_copy(q).wait_send()
 
-        @pl.when(goes_up(q))
-        def _():
-            up_copy(q).wait_send()
-
-        @pl.when(goes_down(q))
-        def _():
-            down_copy(q).wait_send()
+        @pl.when(goes_along(q))
+        def _():
+            along_copy(q).wait_send()
 
 
 def shards(dens_real, dens_imag, upper_band, pattern):
@@ -523,14 +567,18 @@
             pltpu.VMEM((2, NG, W, 3 * W), BF16),
             pltpu.VMEM((2, NJ, 3 * W, W), BF16),
             pltpu.VMEM((2, 2, W, W), F32),
+            pltpu.VMEM((2, 4, BS, TC), F32),
             dma((9,)),
-            dma((2, 2, 2)),
-            dma((2, 2, 2)),
+            dma((2, 2)),
+            dma((2, 2)),
+            dma((2, 4)),
+            dma((2, 4)),
+            dma((2, 4)),
+            dma((2, 4)),
             dma((2, 2, 2, NG)),
             dma((2, 2, 2, NG)),
             dma((2,)),
             dma((2,)),
-            dma((6,)),
             dma((6,)),
             dma((6,)),
             dma((6,)),

time: 128 us -> 120 us (0.938)
  the two profiles are of different devices: /device:TPU:40 before, /device:TPU:6 now
where the time goes in v3:
time: 120 us
  Pallas kernels  115 us (96%)
  local copies, waits for them, and re-layouts  3.79 us (3%)
    pallas_call x1, Pallas kernels, shards(): pl.pallas_call(kernel, out_shape=pltpu.VMEM((2, TR, TC), F32), in_specs=[...  115 us
    squeeze x1, local copies, waits for them, and re-layouts, shards(): return (out[0], out[1])  2.45 us

profile of v3, /device:TPU:6, one launch (start us, length us, event | category | flops | bytes accessed | tf_op | source)
XLA Modules:
  0.0 119.6 jit_solution(6945764489751656524)
XLA Ops:
  0.6 1.3 %copy.6.pat_ref = s32[8,2]{1,0:T(8,128)} copy(s32[8,2]{0,1:T(2,128)} %param.7) | data formatting | bytes 128 | tf_op args[3]
  2.0 115.2 %heun.1 = f32[2,1024,512]{2,1,0:T(8,128)S(1)} custom-call(f32[1024,512]{1,0:T(8,128)} %a_ref.1, f32[1024,512]{1,0:T(8,128)} %b_ref.1, f32[1024,384]{1,0:T(8,128)} %u_ref.1, s32[8,2]{1,0:T(8,128)} %copy.6.pat_ref), custom_call_target="tpu_custom_call" | custom-call | tf_op jit(solution)/shard_map/heun/pallas_call | solution.py:555
  117.2 2.4 %slice_bitcast_fusion = (f32[1024,512]{1,0:T(8,128)}, f32[1024,512]{1,0:T(8,128)}) fusion(f32[2,1024,512]{2,1,0:T(8,128)S(1)} %heun.1), kind=kLoop, calls=%fused_computation | loop fusion | bytes 8388608 | tf_op jit(solution)/shard_map/squeeze | solution.py:591

commit v4 on v3

--- a/solution.py
+++ b/solution.py
@@ -34,7 +34,7 @@
 
 
 def kernel(a_ref, b_ref, u_ref, pat_ref, dens, grad, xs, rowbuf, colbuf, ext, band, hrow, ncol, relay, zrelay,
-           lsem, rs_s, rs_r, bs_s, bs_r, bz_s, bz_r, cs_s, cs_r, ab_s, ab_r, al_s, cr_s, bd_r, rl_s, rl_r):
+           lsem, rs_s, rs_r, bs_s, bs_r, bz_s, bz_r, cs_s, cs_r, ab_s, ab_r, sw_s, bk_s, al_s, cr_s, bd_r, rl_s, rl_r):
     r, c = lax.axis_index("row"), lax.axis_index("col")
     even, core = r % 2 == 0, c % 2
     k = c // 2
@@ -52,11 +52,12 @@
     has_y = (cy_col >= 0) & (cy_col < COLS)
     hub = (c == 7) | (c == 8)
     mine = jnp.minimum(c, COLS - 1 - c)
-    is_relay = (mine % 2 == 0) & (mine < 6)
-    relay_turn = jnp.where(mine == 0, 1, jnp.where(mine == 4, 2, 3))
+    is_relay = mine < 6
+    relay_n = mine % 2
+    relay_turn = jnp.where(mine < 2, 1, jnp.where(mine < 4, 3, 2))
     relay_to = jnp.where(c < 8, 8, 7)
     z_up, z_dn = (r + 2) % ROWS, (r + 6) % ROWS
-    z_next = jnp.where(step_up, z_up, z_dn)
+    z_next, z_back = jnp.where(step_up, z_up, z_dn), jnp.where(step_up, z_dn, z_up)
     depth = jnp.where(even, z, 3 - z)
     first_far = depth
     z_relay = jnp.where(even, z_dn, z_up)
@@ -107,8 +108,8 @@
             def _():
                 b_first(s, i).start()
 
-    def b_near(s):
-        for i in range(3):
+    def b_near(s, pieces=(0, 1, 2)):
+        for i in pieces:
 
             @pl.when(has_b & (i < first_far))
             def _():
@@ -130,25 +131,37 @@
     def hub_copy(s, n, t):
         g = order(0, t)
         src = (a_ref, b_ref)[n] if s == 0 else grad.at[n]
-        near_col = jnp.where(t == 1, 0, jnp.where(t == 2, 4, 2))
+        turn = t if s == 0 else jnp.where(t == 0, 3, t)
+        near_col = jnp.where(turn == 1, 0, jnp.where(turn == 2, 4, 2)) + n
         to = jnp.where(c < 8, near_col, COLS - 1 - near_col)
-        return remote(src.at[pl.ds(mult(g * W), W), pl.ds(col_src[1], W)], relay.at[s, n], cs_s.at[s, 1, n, g], rl_r.at[s, n], (r, to))
-
-    def relay_copy(s, n):
-        g = order(0, relay_turn)
-        return remote(relay.at[s, n], colbuf.at[s, 1, n, pl.ds(mult(g * W), W), :], rl_s.at[s, n], cs_r.at[s, 1, n, g], (r, relay_to))
-
-    def pass_on(s, turns):
-        @pl.when(is_relay & ((relay_turn == 3) == (turns == 3)))
-        def _():
-            for n in range(2):
-                hub_copy(s, n, 1).wait_recv()
-            for n in range(2):
-                relay_copy(s, n).start()
+        return remote(src.at[pl.ds(mult(g * W), W), pl.ds(col_src[1], W)], relay.at[s], cs_s.at[s, 1, n, g], rl_r.at[s], (r, to))
+
+    def relay_copy(s):
+        g = order(0, relay_turn if s == 0 else relay_turn % 3)
+        return remote(relay.at[s], colbuf.at[s, 1, relay_n, pl.ds(mult(g * W), W), :], rl_s.at[s], cs_r.at[s, 1, relay_n, g], (r, relay_to))
+
+    def pass_on(s, which):
+        @pl.when(is_relay & which)
+        def _():
+            hub_copy(s, 0, 1).wait_recv()
+            relay_copy(s).start()
 
     def above_copy(q):
         r0, nr, c0, nc = PIECES[q]
         return remote(ext.at[TR + r0 : TR + r0 + nr, c0 : c0 + nc], ext.at[r0 : r0 + nr, c0 : c0 + nc], ab_s.at[q], ab_r.at[q], (jnp.minimum(r + 1, ROWS - 1), c))
+
+    def swap_copy(q):
+        return remote(piece(ext, q), piece(ext, q), sw_s.at[q], ab_r.at[q], (r, cc_col))
+
+    def take_above():
+        for q in LATE:
+
+            @pl.when(core == q)
+            def _():
+                above_copy(q).wait_recv()
+                swap_copy(q).start()
+                above_copy(1 - q).wait_recv()
+
 
     def piece(ref, q, off=0):
         if isinstance(q, int) and q in LATE:
@@ -163,7 +176,7 @@
         return (dist - part(q) + 4) % 4
 
     def goes_along(q):
-        return jnp.where(near, dist, hops(q)) < 3
+        return jnp.where(near, dist + 1, hops(q)) < 3
 
     def goes_across(q):
         return near & (dist == part(q))
@@ -174,7 +187,14 @@
     def across_copy(q):
         return remote(piece(band, q), piece(band, q), cr_s.at[q], bd_r.at[q], (a_row, c))
 
+    def back_copy(q):
+        return remote(piece(band, q), piece(band, q), bk_s.at[q], bd_r.at[q], (z_back, c))
+
     def along(q):
+        @pl.when(is_src)
+        def _():
+            back_copy(q).start()
+
         @pl.when(goes_along(q))
         def _():
             along_copy(q).start()
@@ -235,7 +255,7 @@
 
     @pl.when(hub)
     def _():
-        for col in (0, 2, 4, 11, 13, 15):
+        for col in (*range(6), *range(10, COLS)):
             greet((r, col))
 
     @pl.when(is_relay)
@@ -243,15 +263,16 @@
         for col in (7, 8):
             greet((r, col))
 
-    pl.semaphore_wait(barrier, 4 + has_b.astype(jnp.int32) + has_y.astype(jnp.int32) + jnp.where(hub, 6, 0) + jnp.where(is_relay, 2, 0))
-
-    @pl.when(last)
-    def _():
-        for q in LATE:
+    pl.semaphore_wait(barrier, 4 + has_b.astype(jnp.int32) + has_y.astype(jnp.int32) + jnp.where(hub, 12, 0) + jnp.where(is_relay, 2, 0))
+
+    for q in LATE:
+
+        @pl.when(last & (core == q))
+        def _():
             above_copy(q).start()
 
     def start_b():
-        pass_on(0, 1)
+        pass_on(0, relay_turn < 3)
         b_near(0)
         b_pass(0)
 
@@ -260,13 +281,18 @@
         own_piece(2).wait()
         across_copy(2).start()
 
+    def hub_direct():
+        @pl.when(hub)
+        def _():
+            for n in range(2):
+                col_copy(0, 1, n, g_a).start()
+
     row_copy(0, 0).start()
 
     @pl.when(jnp.logical_not(near))
     def _():
+        hub_direct()
         row_copy(0, 1).start()
-
-    b_far(0)
 
     @pl.when(is_src)
     def _():
@@ -275,17 +301,19 @@
             along(q)
         along(2)
 
+    b_far(0)
+
     def start_cols(s, t):
         g = order(0, t)
         for n in range(2):
             col_copy(s, 0, n, g).start()
 
-        @pl.when(has_y & (jnp.logical_not(hub) | (t == 0)))
+        @pl.when(has_y & (jnp.logical_not(hub) | ((t == 3) & (s == 1))))
         def _():
             for n in range(2):
                 col_copy(s, 1, n, g).start()
 
-        @pl.when(hub & (t > 0))
+        @pl.when(hub & (t > 0 if s == 0 else t < 3))
         def _():
             for n in range(2):
                 hub_copy(s, n, t).start()
@@ -326,8 +354,7 @@
     def _():
         @pl.when(first)
         def _():
-            for q in LATE:
-                above_copy(q).wait_recv()
+            take_above()
 
         for q in LATE:
             own_piece(q).start()
@@ -335,6 +362,7 @@
             own_piece(q).wait()
             forward(q)
         row_copy(0, 1).start()
+        hub_direct()
         start_b()
 
     @pl.when(jnp.logical_not(is_src))
@@ -347,12 +375,13 @@
             @pl.when(goes_across(q))
             def _():
                 row_copy(0, 1).start()
+                hub_direct()
 
             @pl.when(e == jnp.where(near, 2, 0))
             def _():
                 start_b()
 
-            @pl.when(e == jnp.where(near, 3, dist))
+            @pl.when(e == jnp.where(near, 3, jnp.minimum(dist + 1, 3)))
             def _():
                 for p in LATE:
                     along_copy(p).wait_recv()
@@ -360,10 +389,9 @@
 
         @pl.when(first)
         def _():
-            for q in LATE:
-                above_copy(q).wait_recv()
-
-    pass_on(0, 3)
+            take_above()
+
+    pass_on(0, relay_turn == 3)
 
     @pl.loop(0, TR // BS)
     def _(i):
@@ -492,10 +520,11 @@
                 @pl.when(t == 3)
                 def _():
                     b_far(1)
-                    pass_on(1, 1)
-                    b_near(1)
+                    pass_on(1, relay_turn != 2)
+                    b_near(1, (0,))
+                    pass_on(1, relay_turn == 2)
+                    b_near(1, (1, 2))
                     b_pass(1)
-                    pass_on(1, 3)
 
     @pl.when(has_b)
     def _():
@@ -530,19 +559,27 @@
     @pl.when(is_relay)
     def _():
         for s in range(2):
-            for n in range(2):
-                relay_copy(s, n).wait_send()
-
-    @pl.when(last)
-    def _():
-        for q in LATE:
+            relay_copy(s).wait_send()
+
+    for q in LATE:
+
+        @pl.when(last & (core == q))
+        def _():
             above_copy(q).wait_send()
 
+        @pl.when(first & (core == q))
+        def _():
+            swap_copy(q).wait_send()
+
     for q in range(6):
 
         @pl.when(goes_across(q))
         def _():
             across_copy(q).wait_send()
+
+        @pl.when(is_src)
+        def _():
+            back_copy(q).wait_send()
 
         @pl.when(goes_along(q))
         def _():
@@ -566,7 +603,7 @@
             pltpu.VMEM((TC + W, 3 * BS), F32),
             pltpu.VMEM((2, NG, W, 3 * W), BF16),
             pltpu.VMEM((2, NJ, 3 * W, W), BF16),
-            pltpu.VMEM((2, 2, W, W), F32),
+            pltpu.VMEM((2, W, W), F32),
             pltpu.VMEM((2, 4, BS, TC), F32),
             dma((9,)),
             dma((2, 2)),
@@ -579,11 +616,13 @@
             dma((2, 2, 2, NG)),
             dma((2,)),
             dma((2,)),
+            dma((2,)),
             dma((6,)),
             dma((6,)),
             dma((6,)),
-            dma((2, 2)),
-            dma((2, 2)),
+            dma((6,)),
+            dma((2,)),
+            dma((2,)),
         ],
         compiler_params=pltpu.CompilerParams(collective_id=0, has_side_effects=True, vmem_limit_bytes=55 << 20),
         name="heun",

time: 120 us -> 115 us (0.958)
  Pallas kernels: 115 us -> 109 us
    pallas_call x1, Pallas kernels: 115 us -> 109 us  [shards(): pl.pallas_call(kernel, out_shape=pltpu.VMEM((2, TR, TC), F32), in_specs=[...]
where the time goes in v4:
time: 115 us; the launch traced here: 114 us
  Pallas kernels  109 us (95%)
  local copies, waits for them, and re-layouts  3.79 us (3%)
    pallas_call x1, Pallas kernels, shards(): pl.pallas_call(kernel, out_shape=pltpu.VMEM((2, TR, TC), F32), in_specs=[...  109 us
    squeeze x1, local copies, waits for them, and re-layouts, shards(): return (out[0], out[1])  2.45 us

profile of v4, /device:TPU:6, one launch (start us, length us, event | category | flops | bytes accessed | tf_op | source)
XLA Modules:
  0.0 113.8 jit_solution(10813235606102859081)
XLA Ops:
  0.6 1.3 %copy.6.pat_ref = s32[8,2]{1,0:T(8,128)} copy(s32[8,2]{0,1:T(2,128)} %param.7) | data formatting | bytes 128 | tf_op args[3]
  2.0 109.3 %heun.1 = f32[2,1024,512]{2,1,0:T(8,128)S(1)} custom-call(f32[1024,512]{1,0:T(8,128)} %a_ref.1, f32[1024,512]{1,0:T(8,128)} %b_ref.1, f32[1024,384]{1,0:T(8,128)} %u_ref.1, s32[8,2]{1,0:T(8,128)} %copy.6.pat_ref), custom_call_target="tpu_custom_call" | custom-call | tf_op jit(solution)/shard_map/heun/pallas_call | solution.py:592
  111.3 2.4 %slice_bitcast_fusion = (f32[1024,512]{1,0:T(8,128)}, f32[1024,512]{1,0:T(8,128)}) fusion(f32[2,1024,512]{2,1,0:T(8,128)S(1)} %heun.1), kind=kLoop, calls=%fused_computation | loop fusion | bytes 8388608 | tf_op jit(solution)/shard_map/squeeze | solution.py:630

commit v5 on v4

--- a/solution.py
+++ b/solution.py
@@ -34,7 +34,7 @@
 
 
 def kernel(a_ref, b_ref, u_ref, pat_ref, dens, grad, xs, rowbuf, colbuf, ext, band, hrow, ncol, relay, zrelay,
-           lsem, rs_s, rs_r, bs_s, bs_r, bz_s, bz_r, cs_s, cs_r, ab_s, ab_r, sw_s, bk_s, al_s, cr_s, bd_r, rl_s, rl_r):
+           lsem, rs_s, rs_r, bs_s, bs_r, bz_s, bz_r, cs_s, cs_r, ab_s, ab_r, sw_s, mt_s, bk_s, al_s, cr_s, bd_r, rl_s, rl_r):
     r, c = lax.axis_index("row"), lax.axis_index("col")
     even, core = r % 2 == 0, c % 2
     k = c // 2
@@ -175,11 +175,21 @@
     def hops(q):
         return (dist - part(q) + 4) % 4
 
+    def travels(q):
+        return core == 0 if isinstance(q, int) and q in LATE else True
+
     def goes_along(q):
-        return jnp.where(near, dist + 1, hops(q)) < 3
+        return (jnp.where(near, dist + 1, hops(q)) < 3) & travels(q)
 
     def goes_across(q):
-        return near & (dist == part(q))
+        return near & (dist == part(q)) & travels(q)
+
+    def goes_back(q):
+        return is_src & travels(q)
+
+    def mate_copy(p):
+        r0, nr, c0, nc = PIECES[p]
+        return remote(band.at[r0 + 4 * BS : r0 + 4 * BS + nr, c0 : c0 + nc], piece(band, p), mt_s.at[p], bd_r.at[p], (r, cc_col))
 
     def along_copy(q):
         return remote(piece(band, q), piece(band, q), al_s.at[q], bd_r.at[q], (z_next, c))
@@ -191,7 +201,7 @@
         return remote(piece(band, q), piece(band, q), bk_s.at[q], bd_r.at[q], (z_back, c))
 
     def along(q):
-        @pl.when(is_src)
+        @pl.when(goes_back(q))
         def _():
             back_copy(q).start()
 
@@ -244,7 +254,7 @@
     def _(i):
         rows = pl.ds(mult(W + i * BS, BS), BS)
         for d in range(1, KB + 1):
-            present = (pat_ref[i, d - 1] > 0) & (r * (TR // BS) + i + d < NB)
+            present = (pat_ref[d - 1, i] > 0) & (r * (TR // BS) + i + d < NB)
             cols = slice(d * BS, (d + 1) * BS)
             ext[rows, cols] = ext[rows, cols] * jnp.where(present, 1.0, 0.0).astype(F32)
 
@@ -381,11 +391,16 @@
             def _():
                 start_b()
 
-            @pl.when(e == jnp.where(near, 3, jnp.minimum(dist + 1, 3)))
+            @pl.when((core == 0) & (e == jnp.where(near, 3, jnp.minimum(dist + 1, 3))))
             def _():
                 for p in LATE:
                     along_copy(p).wait_recv()
                     forward(p)
+
+        @pl.when(core == 0)
+        def _():
+            for p in LATE:
+                mate_copy(p).start()
 
         @pl.when(first)
         def _():
@@ -409,6 +424,11 @@
             value = u if d > 0 else u.T if d < 0 else 0.5 * (u + u.T)
             put(h + d + KB, value)
         put((1 - h) * (2 * KB + 1), jnp.zeros((BS, BS), F32))
+
+    @pl.when(jnp.logical_not(is_src) & (core == 1))
+    def _():
+        for p in LATE:
+            mate_copy(p).wait_recv()
 
     @pl.loop(0, TC // BS)
     def _(i):
@@ -474,57 +494,75 @@
         rows = pl.ds(mult(g * W), W)
         dens[1 - n, rows, :] += (-0.5 if n == 0 else 0.5) * jnp.dot(lhs, rhs, preferred_element_type=F32)
 
-    for s in range(2):
-
-        @pl.loop(0, NG)
-        def _(t):
-            g = order(s, t)
-            take_cols(s, 0, g)
-
-            @pl.when(has_y)
-            def _():
-                take_cols(s, 1, g)
-
-            @pl.when(t == 2 * s)
-            def _():
-                take_rows(s, 0)
-
-            if s == 0:
-
-                @pl.when((t == 3) & has_b)
-                def _():
-                    take_rows(s, 1)
-
-            @pl.loop(0, 2 * NJ)
-            def _(i):
-                n, j = i // NJ, i % NJ
-                value = product(s, n, g, j)
-                rows, cols = pl.ds(mult(g * W), W), pl.ds(mult(j * W), W)
-                if s == 0:
-                    grad[n, rows, cols] = value
-                    hi, lo = split(value)
-                    xs[1, n, 0, pl.ds(mult(W + g * W), W), pl.ds(mult(W + j * W), W)] = hi
-                    xs[1, n, 1, pl.ds(mult(W + g * W), W), pl.ds(mult(W + j * W), W)] = lo
-                else:
-                    dens[n, rows, cols] = dens[n, rows, cols] + grad[n, rows, cols] + 0.5 * value
-
-            if s == 0:
-
-                @pl.when(t == 0)
-                def _():
-                    for n in range(2):
-                        row_copy(1, n).start()
-
-                start_cols(1, t)
-
-                @pl.when(t == 3)
-                def _():
-                    b_far(1)
-                    pass_on(1, relay_turn != 2)
-                    b_near(1, (0,))
-                    pass_on(1, relay_turn == 2)
-                    b_near(1, (1, 2))
-                    b_pass(1)
+    @pl.loop(0, NG)
+    def _(t):
+        g = order(0, t)
+        take_cols(0, 0, g)
+
+        @pl.when(has_y)
+        def _():
+            take_cols(0, 1, g)
+
+        @pl.when(t == 0)
+        def _():
+            take_rows(0, 0)
+
+        @pl.when((t == 3) & has_b)
+        def _():
+            take_rows(0, 1)
+
+        @pl.loop(0, 2 * NJ)
+        def _(i):
+            n, j = i // NJ, i % NJ
+            value = product(0, n, g, j)
+            grad[n, pl.ds(mult(g * W), W), pl.ds(mult(j * W), W)] = value
+            hi, lo = split(value)
+            rows, cols = pl.ds(mult(W + g * W), W), pl.ds(mult(W + j * W), W)
+            xs[1, n, 0, rows, cols] = hi
+            xs[1, n, 1, rows, cols] = lo
+
+        @pl.when(t == 0)
+        def _():
+            for n in range(2):
+                row_copy(1, n).start()
+
+        start_cols(1, t)
+
+        @pl.when(t == 3)
+        def _():
+            b_far(1)
+            pass_on(1, relay_turn != 2)
+            b_near(1, (0,))
+            pass_on(1, relay_turn == 2)
+            b_near(1, (1, 2))
+            b_pass(1)
+
+    def finish(g, j):
+        @pl.loop(0, 2)
+        def _(n):
+            rows, cols = pl.ds(mult(g * W), W), pl.ds(mult(j * W), W)
+            dens[n, rows, cols] = dens[n, rows, cols] + grad[n, rows, cols] + 0.5 * product(1, n, g, j)
+
+    @pl.loop(0, NG)
+    def _(t):
+        g = order(1, t)
+        take_cols(1, 0, g)
+
+        @pl.when(t == 2)
+        def _():
+            take_rows(1, 0)
+
+        finish(g, 1 - core)
+
+    @pl.loop(0, NG)
+    def _(t):
+        g = order(1, t)
+
+        @pl.when(has_y)
+        def _():
+            take_cols(1, 1, g)
+
+        finish(g, core)
 
     @pl.when(has_b)
     def _():
@@ -571,13 +609,18 @@
         def _():
             swap_copy(q).wait_send()
 
+    @pl.when(jnp.logical_not(is_src) & (core == 0))
+    def _():
+        for p in LATE:
+            mate_copy(p).wait_send()
+
     for q in range(6):
 
         @pl.when(goes_across(q))
         def _():
             across_copy(q).wait_send()
 
-        @pl.when(is_src)
+        @pl.when(goes_back(q))
         def _():
             back_copy(q).wait_send()
 
@@ -617,6 +660,7 @@
             dma((2,)),
             dma((2,)),
             dma((2,)),
+            dma((2,)),
             dma((6,)),
             dma((6,)),
             dma((6,)),
@@ -626,7 +670,7 @@
         ],
         compiler_params=pltpu.CompilerParams(collective_id=0, has_side_effects=True, vmem_limit_bytes=55 << 20),
         name="heun",
-    )(dens_real, dens_imag, upper_band, pattern)
+    )(dens_real, dens_imag, upper_band, pattern.T)
     return out[0], out[1]
 
 

time: 115 us -> 113 us (0.983)
  local copies, waits for them, and re-layouts: 3.79 us -> 2.45 us
    unnamed x1 -> x0, local copies, waits for them, and re-layouts: 1.35 us -> none
where the time goes in v5:
time: 113 us; the launch traced here: 112 us
  Pallas kernels  109 us (96%)
  local copies, waits for them, and re-layouts  2.45 us (2%)
    pallas_call x1, Pallas kernels, shards(): pl.pallas_call(kernel, out_shape=pltpu.VMEM((2, TR, TC), F32), in_specs=[...  109 us
    squeeze x1, local copies, waits for them, and re-layouts, shards(): return (out[0], out[1])  2.45 us

profile of v5, /device:TPU:6, one launch (start us, length us, event | category | flops | bytes accessed | tf_op | source)
XLA Modules:
  0.0 112.5 jit_solution(7762844217625544002)
XLA Ops:
  0.6 109.4 %heun.1 = f32[2,1024,512]{2,1,0:T(8,128)S(1)} custom-call(f32[1024,512]{1,0:T(8,128)} %a_ref.1, f32[1024,512]{1,0:T(8,128)} %b_ref.1, f32[1024,384]{1,0:T(8,128)} %u_ref.1, s32[2,8]{1,0:T(2,128)} %bitcast.5), custom_call_target="tpu_custom_call" | custom-call | tf_op jit(solution)/shard_map/heun/pallas_call | solution.py:635
  110.0 2.4 %slice_bitcast_fusion = (f32[1024,512]{1,0:T(8,128)}, f32[1024,512]{1,0:T(8,128)}) fusion(f32[2,1024,512]{2,1,0:T(8,128)S(1)} %heun.1), kind=kLoop, calls=%fused_computation | loop fusion | bytes 8388608 | tf_op jit(solution)/shard_map/squeeze | solution.py:674

commit v6 on v5

--- a/solution.py
+++ b/solution.py
@@ -56,6 +56,7 @@
     relay_n = mine % 2
     relay_turn = jnp.where(mine < 2, 1, jnp.where(mine < 4, 3, 2))
     relay_to = jnp.where(c < 8, 8, 7)
+    urgent = is_src | (r + 1 == k) | (r + 1 == k + 1 - 2 * (k % 2))
     z_up, z_dn = (r + 2) % ROWS, (r + 6) % ROWS
     z_next, z_back = jnp.where(step_up, z_up, z_dn), jnp.where(step_up, z_dn, z_up)
     depth = jnp.where(even, z, 3 - z)
@@ -248,15 +249,20 @@
     def _():
         ext[0:W, :] = jnp.zeros((W, 3 * BS), F32)
 
-    loads[2].wait()
-
-    @pl.loop(0, TR // BS)
-    def _(i):
-        rows = pl.ds(mult(W + i * BS, BS), BS)
-        for d in range(1, KB + 1):
-            present = (pat_ref[d - 1, i] > 0) & (r * (TR // BS) + i + d < NB)
-            cols = slice(d * BS, (d + 1) * BS)
-            ext[rows, cols] = ext[rows, cols] * jnp.where(present, 1.0, 0.0).astype(F32)
+    def prepare():
+        loads[2].wait()
+
+        @pl.loop(0, TR // BS)
+        def _(i):
+            rows = pl.ds(mult(W + i * BS, BS), BS)
+            for d in range(1, KB + 1):
+                present = (pat_ref[d - 1, i] > 0) & (r * (TR // BS) + i + d < NB)
+                cols = slice(d * BS, (d + 1) * BS)
+                ext[rows, cols] = ext[rows, cols] * jnp.where(present, 1.0, 0.0).astype(F32)
+
+    @pl.when(urgent)
+    def _():
+        prepare()
 
     @pl.when(is_src)
     def _():
@@ -275,11 +281,16 @@
 
     pl.semaphore_wait(barrier, 4 + has_b.astype(jnp.int32) + has_y.astype(jnp.int32) + jnp.where(hub, 12, 0) + jnp.where(is_relay, 2, 0))
 
-    for q in LATE:
-
-        @pl.when(last & (core == q))
-        def _():
-            above_copy(q).start()
+    def start_above():
+        for q in LATE:
+
+            @pl.when(last & (core == q))
+            def _():
+                above_copy(q).start()
+
+    @pl.when(urgent)
+    def _():
+        start_above()
 
     def start_b():
         pass_on(0, relay_turn < 3)
@@ -331,6 +342,11 @@
     @pl.loop(0, NG)
     def _(t):
         start_cols(0, t)
+
+    @pl.when(jnp.logical_not(urgent))
+    def _():
+        prepare()
+        start_above()
 
     def clear_rows(s):
         for n in range(2):
@@ -375,6 +391,32 @@
         hub_direct()
         start_b()
 
+    def build_rows():
+        @pl.loop(0, TR // BS)
+        def _(i):
+            g, h = i // 2, i % 2
+            rows = pl.ds(mult(h * BS, BS), BS)
+
+            def put(pos, value):
+                hi, lo = split(value * STEP_TIME)
+                cols = pl.ds(mult(pos * BS, BS), BS)
+                hrow[0, g, rows, cols] = hi
+                hrow[1, g, rows, cols] = lo
+
+            for d in range(-KB, KB + 1):
+                u = ext[pl.ds(mult((i + KB + min(d, 0)) * BS, BS), BS), abs(d) * BS : (abs(d) + 1) * BS]
+                value = u if d > 0 else u.T if d < 0 else 0.5 * (u + u.T)
+                put(h + d + KB, value)
+            put((1 - h) * (2 * KB + 1), jnp.zeros((BS, BS), F32))
+
+    @pl.when(jnp.logical_not(near))
+    def _():
+        @pl.when(first)
+        def _():
+            take_above()
+
+        build_rows()
+
     @pl.when(jnp.logical_not(is_src))
     def _():
         for e in range(4):
@@ -391,7 +433,7 @@
             def _():
                 start_b()
 
-            @pl.when((core == 0) & (e == jnp.where(near, 3, jnp.minimum(dist + 1, 3))))
+            @pl.when((core == 0) & (e == jnp.where(near, 3, dist)))
             def _():
                 for p in LATE:
                     along_copy(p).wait_recv()
@@ -402,28 +444,15 @@
             for p in LATE:
                 mate_copy(p).start()
 
-        @pl.when(first)
+        @pl.when(first & near)
         def _():
             take_above()
 
     pass_on(0, relay_turn == 3)
 
-    @pl.loop(0, TR // BS)
-    def _(i):
-        g, h = i // 2, i % 2
-        rows = pl.ds(mult(h * BS, BS), BS)
-
-        def put(pos, value):
-            hi, lo = split(value * STEP_TIME)
-            cols = pl.ds(mult(pos * BS, BS), BS)
-            hrow[0, g, rows, cols] = hi
-            hrow[1, g, rows, cols] = lo
-
-        for d in range(-KB, KB + 1):
-            u = ext[pl.ds(mult((i + KB + min(d, 0)) * BS, BS), BS), abs(d) * BS : (abs(d) + 1) * BS]
-            value = u if d > 0 else u.T if d < 0 else 0.5 * (u + u.T)
-            put(h + d + KB, value)
-        put((1 - h) * (2 * KB + 1), jnp.zeros((BS, BS), F32))
+    @pl.when(near)
+    def _():
+        build_rows()
 
     @pl.when(jnp.logical_not(is_src) & (core == 1))
     def _():
@@ -520,11 +549,11 @@
             rows, cols = pl.ds(mult(W + g * W), W), pl.ds(mult(W + j * W), W)
             xs[1, n, 0, rows, cols] = hi
             xs[1, n, 1, rows, cols] = lo
-
-        @pl.when(t == 0)
-        def _():
-            for n in range(2):
-                row_copy(1, n).start()
+            for m in range(2):
+
+                @pl.when((t == 0) & (i == (m + 1) * NJ - 1))
+                def _():
+                    row_copy(1, m).start()
 
         start_cols(1, t)
 

time: 113 us -> 112 us (level); the launches traced: 112 us -> 110 us
  Pallas kernels: 109 us -> 107 us
    pallas_call x1, Pallas kernels: 109 us -> 107 us  [shards(): pl.pallas_call(kernel, out_shape=pltpu.VMEM((2, TR, TC), F32), in_specs=[...]
where the time goes in v6:
time: 112 us; the launch traced here: 110 us
  Pallas kernels  107 us (96%)
  local copies, waits for them, and re-layouts  2.45 us (2%)
    pallas_call x1, Pallas kernels, shards(): pl.pallas_call(kernel, out_shape=pltpu.VMEM((2, TR, TC), F32), in_specs=[...  107 us
    squeeze x1, local copies, waits for them, and re-layouts, shards(): return (out[0], out[1])  2.45 us

profile of v6, /device:TPU:6, one launch (start us, length us, event | category | flops | bytes accessed | tf_op | source)
XLA Modules:
  0.0 110.3 jit_solution(3820567529785788176)
XLA Ops:
  0.6 107.2 %heun.1 = f32[2,1024,512]{2,1,0:T(8,128)S(1)} custom-call(f32[1024,512]{1,0:T(8,128)} %a_ref.1, f32[1024,512]{1,0:T(8,128)} %b_ref.1, f32[1024,384]{1,0:T(8,128)} %u_ref.1, s32[2,8]{1,0:T(2,128)} %bitcast.5), custom_call_target="tpu_custom_call" | custom-call | tf_op jit(solution)/shard_map/heun/pallas_call | solution.py:664
  107.8 2.4 %slice_bitcast_fusion = (f32[1024,512]{1,0:T(8,128)}, f32[1024,512]{1,0:T(8,128)}) fusion(f32[2,1024,512]{2,1,0:T(8,128)S(1)} %heun.1), kind=kLoop, calls=%fused_computation | loop fusion | bytes 8388608 | tf_op jit(solution)/shard_map/squeeze | solution.py:703

commit v7 on v6

--- a/solution.py
+++ b/solution.py
@@ -511,12 +511,11 @@
         total = jnp.dot(lhs, rhs, preferred_element_type=F32)
         return jnp.where(n == 0, 1.0, -1.0).astype(F32) * total
 
-    def last_part(n):
-        g = NG - 1 - g_a
-        for i in (2 * n, 2 * n + 1):
-            b_direct(1, i).wait_recv()
-        hi, lo = split(rowbuf[1, 1, n])
-        cols = pl.ds(mult(jnp.where(even, 0, 2 * W)), W)
+    def last_part(i):
+        g, n = NG - 1 - g_a, i // 2
+        b_direct(1, i).wait_recv()
+        hi, lo = split(rowbuf[1, 1, n, i % 2 * BS : (i % 2 + 1) * BS, :])
+        cols = pl.ds(mult(jnp.where(even, 0, 2 * W) + i % 2 * BS, BS), BS)
         h_h, h_l = hrow[0, g, :, cols], hrow[1, g, :, cols]
         lhs = jnp.concatenate([h_h, h_h, h_l], axis=1)
         rhs = jnp.concatenate([hi, lo, hi], axis=0)
@@ -593,12 +592,7 @@
 
         finish(g, core)
 
-    @pl.when(has_b)
-    def _():
-        for n in range(2):
-            last_part(n)
-
-    for s in range(2):
+    def sent_rows(s):
         for n in range(2):
             row_copy(s, n).wait_send()
 
@@ -612,6 +606,9 @@
             @pl.when(i > depth)
             def _():
                 b_second(s, i).wait_send()
+
+    sent_rows(0)
+    for s in range(2):
 
         @pl.loop(0, NG)
         def _(g):
@@ -656,6 +653,13 @@
         @pl.when(goes_along(q))
         def _():
             along_copy(q).wait_send()
+
+    @pl.when(has_b)
+    def _():
+        for i in range(4):
+            last_part(i)
+
+    sent_rows(1)
 
 
 def shards(dens_real, dens_imag, upper_band, pattern):

time: 112 us -> 111 us (level)
  no operation moved by 1% of the time
where the time goes in v7:
time: 111 us; the launch traced here: 110 us
  Pallas kernels  107 us (96%)
  local copies, waits for them, and re-layouts  2.45 us (2%)
    pallas_call x1, Pallas kernels, shards(): pl.pallas_call(kernel, out_shape=pltpu.VMEM((2, TR, TC), F32), in_specs=[...  107 us
    squeeze x1, local copies, waits for them, and re-layouts, shards(): return (out[0], out[1])  2.45 us

profile of v7, /device:TPU:6, one launch (start us, length us, event | category | flops | bytes accessed | tf_op | source)
XLA Modules:
  0.0 110.0 jit_solution(9584206777536234377)
XLA Ops:
  0.6 106.9 %heun.1 = f32[2,1024,512]{2,1,0:T(8,128)S(1)} custom-call(f32[1024,512]{1,0:T(8,128)} %a_ref.1, f32[1024,512]{1,0:T(8,128)} %b_ref.1, f32[1024,384]{1,0:T(8,128)} %u_ref.1, s32[2,8]{1,0:T(2,128)} %bitcast.5), custom_call_target="tpu_custom_call" | custom-call | tf_op jit(solution)/shard_map/heun/pallas_call | solution.py:668
  107.6 2.4 %slice_bitcast_fusion = (f32[1024,512]{1,0:T(8,128)}, f32[1024,512]{1,0:T(8,128)}) fusion(f32[2,1024,512]{2,1,0:T(8,128)S(1)} %heun.1), kind=kLoop, calls=%fused_computation | loop fusion | bytes 8388608 | tf_op jit(solution)/shard_map/squeeze | solution.py:707
